TPU v7x, 32 devices: a whole 2x2x4 slice. The times are simulated.
32 devices in a mesh: region: 16 (over z, y, core), tracer: 2 (over x).
Axes of the slice: x: 2, y: 2, z: 4, core: 2. Of those that a mesh axis runs over, the one named last changes fastest.
Arguments:
- tracers: float32 [256, 32, 6144], P('tracer', 'region'), may hold values from 0.2 to 1.5
- fluxes: float32 [2, 32, 6144], P(None, 'region', 'tracer'), may hold values from -0.4 to 0.4
- rate_coeff: float32 [1024], replicated, may hold values from 0.005 to 0.05
- first_reactant: int32 [1024], replicated, may hold values from 0 to 255
- second_reactant: int32 [1024], replicated, may hold values from 0 to 255
- product_species: int32 [1024], replicated, may hold values from 0 to 255
Outputs:
- tracers_out: float32 [256, 32, 6144], P('tracer', 'region')
All inputs are finite; a program needn't handle non-finite values.
Results may differ from a plain program's by a relative error of at most 0.0001.
Values sent between devices are 32-bit elements; how exact they have to be, the bound alone decides.
A program may use at most 128 MiB of HBM per device.

v0:
```python
import functools

import jax
import jax.numpy as jnp
from jax import lax
from jax.experimental import pallas as pl
from jax.experimental.pallas import tpu as pltpu
from jax.sharding import PartitionSpec as P

NY = 48
SUBSTEPS = 4
LANES = 128
BLOCKS = 3
COLUMNS = 2
ROWS = COLUMNS * BLOCKS
GROUP = BLOCKS * LANES
PITCH = 9
MESH = pl.DeviceIdType.MESH


def south_of(values, lane):
    shifted = []
    for t in range(BLOCKS):
        source = values[t] if t == 0 else jnp.where(lane == LANES - 1, values[t - 1], values[t])
        shifted.append(pltpu.roll(source, 1, 1))
    return shifted


def north_of(values, lane):
    shifted = []
    for t in range(BLOCKS):
        last = t == BLOCKS - 1
        source = values[t] if last else jnp.where(lane == 0, values[t + 1], values[t])
        shifted.append(pltpu.roll(source, LANES - 1, 1))
    return shifted


def up(values):
    return jnp.maximum(values, 0.0)


def down(values):
    return jnp.minimum(values, 0.0)


def write_coefficients(groups, coef_ref, own_ref, west_ref, east_ref):
    lane = lax.broadcasted_iota(jnp.int32, (groups, LANES), 1)

    def read(ref, axis, column):
        rows = ref.reshape(2 * groups * ROWS, LANES)
        return [
            rows[pl.ds(axis * groups * ROWS + t * COLUMNS + column, groups, stride=ROWS), :]
            for t in range(BLOCKS)
        ]

    sources = ((west_ref, 1), (own_ref, 0), (own_ref, 1), (east_ref, 0), (east_ref, 1))
    u = [read(ref, 0, column) for ref, column in sources]
    for at in range(4):
        v = read(sources[at][0], 1, sources[at][1])
        above = north_of(v, lane)
        for t in range(BLOCKS):
            y = (lane + t * LANES) % NY
            bottom, top = y == 0, y == NY - 1
            west_face, east_face = u[at][t], u[at + 1][t]
            center = (
                1.0
                + down(west_face)
                - up(east_face)
                + jnp.where(bottom, 0.0, down(v[t]))
                - jnp.where(top, 0.0, up(above[t]))
            )
            south = jnp.where(bottom, 0.0, up(v[t]))
            north = jnp.where(top, 0.0, -down(above[t]))
            for m, value in enumerate((center, up(west_face), -down(east_face), south, north)):
                coef_ref[(at * BLOCKS + t) * 5 + m, pl.ds(0, groups), :] = value


def kernel(
    parts,
    count,
    groups,
    first_ref,
    second_ref,
    rate_ref,
    table_ref,
    flux_ref,
    nat_ref,
    out_ref,
    own_ref,
    west_ref,
    east_ref,
    stage_ref,
    flux_own,
    flux_west,
    flux_east,
    coef_ref,
    c_ref,
    w_ref,
    x_send,
    x_recv,
    w_send,
    w_recv,
    e_send,
    e_recv,
    r_send,
    r_recv,
    load_sem,
    save_sem,
    f_send,
    f_recv,
    f_load,
):
    region, me = lax.axis_index("region"), lax.axis_index("tracer")
    ring = lax.axis_size("region")
    east, west = (region + 1) % ring, (region + ring - 1) % ring
    reactions = first_ref.shape[0]
    species = parts * count
    rows = count * ROWS

    def partner(shift):
        return (me + shift) % parts

    barrier = pltpu.get_barrier_semaphore()
    for shift in range(1, parts):
        pl.semaphore_signal(barrier, 1, device_id=(region, partner(shift)), device_id_type=MESH)
    for side in (east, west):
        pl.semaphore_signal(barrier, 1, device_id=(side, me), device_id_type=MESH)
    pl.semaphore_wait(barrier, parts + 1)

    def remote(source, target, send, recv, device):
        return pltpu.make_async_remote_copy(
            src_ref=source,
            dst_ref=target,
            send_sem=send,
            recv_sem=recv,
            device_id=device,
            device_id_type=MESH,
        )

    def flux_east_copy():
        return remote(flux_ref, flux_west, f_send.at[0], f_recv.at[0], (east, me))

    def flux_west_copy():
        return remote(flux_ref, flux_east, f_send.at[1], f_recv.at[1], (west, me))

    def load(g):
        return pltpu.make_async_copy(nat_ref.at[:, me * groups + g], own_ref.at[0, g], load_sem.at[g])

    def exchange(shift, g):
        owner = partner(shift)
        return remote(
            nat_ref.at[:, owner * groups + g],
            own_ref.at[shift, g],
            x_send.at[shift, g],
            x_recv.at[shift, g],
            (region, owner),
        )

    def halo(part, g):
        source = nat_ref.at[:, me * groups + g] if part == 0 else own_ref.at[part, g]
        return (
            remote(source, west_ref.at[part, g], w_send.at[part, g], w_recv.at[part, g], (east, me)),
            remote(source, east_ref.at[part, g], e_send.at[part, g], e_recv.at[part, g], (west, me)),
        )

    def give_back(shift, g):
        return remote(
            stage_ref.at[shift, g],
            out_ref.at[:, me * groups + g],
            r_send.at[shift, g],
            r_recv.at[shift, g],
            (region, (me + parts - shift) % parts),
        )

    def save(g):
        return pltpu.make_async_copy(stage_ref.at[0, g], out_ref.at[:, me * groups + g], save_sem.at[g])

    def send_halo(part, g):
        for copy in halo(part, g):
            copy.start()

    def pass_on(g):
        for shift in range(1, parts):
            exchange(shift, g).wait_recv()
            send_halo(shift, g)

    flux_load = pltpu.make_async_copy(flux_ref, flux_own, f_load)
    flux_load.start()
    flux_east_copy().start()
    flux_west_copy().start()
    for g in range(groups):
        for shift in range(1, parts):
            exchange(shift, g).start()
        if g < 2:
            send_halo(0, g)
    for g in range(groups):
        load(g).start()
    c_ref[...] = jnp.zeros_like(c_ref)
    flux_load.wait()
    flux_east_copy().wait()
    flux_west_copy().wait()
    write_coefficients(groups, coef_ref, flux_own, flux_west, flux_east)
    for g in range(2):
        if g < groups:
            pass_on(g)
        if g + 2 < groups:
            send_halo(0, g + 2)

    lane = lax.broadcasted_iota(jnp.int32, (8, LANES), 1)
    unroll = 16

    def one_group(g, carry):
        @pl.when(g + 2 < groups)
        def _():
            pass_on(g + 2)

        @pl.when(g + 4 < groups)
        def _():
            send_halo(0, g + 4)

        load(g).wait()
        for part in range(parts):
            for copy in halo(part, g):
                copy.wait_recv()

        def coefficient(at, t, m):
            return coef_ref[(at * BLOCKS + t) * 5 + m, pl.ds(g, 8, stride=0), :]

        def step(cols, at):
            south, north = south_of(cols[1], lane), north_of(cols[1], lane)
            return [
                coefficient(at, t, 0) * cols[1][t]
                + coefficient(at, t, 1) * cols[0][t]
                + coefficient(at, t, 2) * cols[2][t]
                + coefficient(at, t, 3) * south[t]
                + coefficient(at, t, 4) * north[t]
                for t in range(BLOCKS)
            ]

        for part in range(parts):

            def advect(i, carry, part=part):
                def read(ref, column):
                    flat = ref.at[part, g].reshape(rows, LANES)
                    return [
                        flat[pl.ds(i * (8 * ROWS) + t * COLUMNS + column, 8, stride=ROWS), :]
                        for t in range(BLOCKS)
                    ]

                cols = [read(ref, column) for ref in (west_ref, own_ref, east_ref) for column in range(2)]
                mid = [step(cols[at : at + 3], at) for at in range(4)]
                for column in range(COLUMNS):
                    new = step(mid[column : column + 3], column + 1)
                    for t in range(BLOCKS):
                        start = (part * count + i * 8) * PITCH + t * COLUMNS + column
                        c_ref[pl.ds(start, 8, stride=PITCH), :] = new[t]
                return carry

            lax.fori_loop(0, count // 8, advect, 0)

        def react(repeat, carry):
            def velocities(i, carry):
                for j in range(unroll):
                    r = i * unroll + j
                    w_ref[pl.ds(r * PITCH, 8), :] = (
                        rate_ref[r]
                        * c_ref[pl.ds(first_ref[r], 8), :]
                        * c_ref[pl.ds(second_ref[r], 8), :]
                    )
                return carry

            lax.fori_loop(0, reactions // unroll, velocities, 0)

            for k in range(ROWS):
                w = w_ref[pl.ds(k, reactions, stride=PITCH), :]
                high = w.astype(jnp.bfloat16)
                low = (w - high.astype(jnp.float32)).astype(jnp.bfloat16)
                change = jnp.dot(
                    table_ref[...],
                    jnp.concatenate([high, low], axis=1),
                    preferred_element_type=jnp.float32,
                )
                where = pl.ds(k, species, stride=PITCH)
                c_ref[where, :] = c_ref[where, :] + (change[:, :LANES] + change[:, LANES:])
            return carry

        lax.fori_loop(0, SUBSTEPS, react, 0)

        for part in range(parts):

            def put(i, carry, part=part):
                flat = stage_ref.at[part, g].reshape(rows, LANES)
                for k in range(ROWS):
                    start = (part * count + i * 8) * PITCH + k
                    flat[pl.ds(i * (8 * ROWS) + k, 8, stride=ROWS), :] = c_ref[
                        pl.ds(start, 8, stride=PITCH), :
                    ]
                return carry

            lax.fori_loop(0, count // 8, put, 0)
        for shift in range(1, parts):
            give_back(shift, g).start()
        save(g).start()
        return carry

    lax.fori_loop(0, groups, one_group, 0)

    def finish(g, carry):
        save(g).wait()
        for shift in range(1, parts):
            exchange(shift, g).wait_send()
            give_back(shift, g).wait()
        for part in range(parts):
            for copy in halo(part, g):
                copy.wait_send()
        return carry

    lax.fori_loop(0, groups, finish, 0)


def body(tracers, fluxes, rate_coeff, first_reactant, second_reactant, product_species):
    parts = lax.axis_size("tracer")
    me = lax.axis_index("tracer")
    count, columns, length = tracers.shape
    total = length // GROUP
    groups = total // parts
    species = parts * count
    reactions = rate_coeff.shape[0]

    def by_block(values):
        lead = values.shape[0]
        blocks = values.shape[2] // LANES
        return (
            values.reshape(lead, columns, blocks, LANES)
            .transpose(0, 2, 1, 3)
            .reshape(lead, blocks // BLOCKS, BLOCKS, columns, LANES)
        )

    natural = by_block(tracers)
    wind = by_block(fluxes)

    def place(index):
        return (me - index // count) % parts * count + index % count

    order = jnp.arange(species, dtype=jnp.int32)[:, None]
    first, second, product = (
        place(index) for index in (first_reactant, second_reactant, product_species)
    )
    table = (
        (product[None, :] == order).astype(jnp.float32)
        - (first[None, :] == order).astype(jnp.float32)
        - (second[None, :] == order).astype(jnp.float32)
    ).astype(jnp.bfloat16)

    smem = pl.BlockSpec(memory_space=pltpu.SMEM)
    vmem = pl.BlockSpec(memory_space=pltpu.VMEM)
    anywhere = pl.BlockSpec(memory_space=pl.ANY)
    slab = (parts, groups, count, BLOCKS, columns, LANES)
    dma = pltpu.SemaphoreType.DMA
    out = pl.pallas_call(
        functools.partial(kernel, parts, count, groups),
        out_shape=jax.ShapeDtypeStruct(natural.shape, jnp.float32),
        in_specs=[smem] * 3 + [vmem] + [anywhere] * 2,
        out_specs=anywhere,
        scratch_shapes=[pltpu.VMEM(slab, jnp.float32)] * 4
        + [pltpu.VMEM(wind.shape, jnp.float32)] * 3
        + [
            pltpu.VMEM((4 * BLOCKS * 5, -(-groups // 8) * 8, LANES), jnp.float32),
            pltpu.VMEM((species * PITCH + 8, LANES), jnp.float32),
            pltpu.VMEM((reactions * PITCH + 8, LANES), jnp.float32),
        ]
        + [dma((parts, groups))] * 8
        + [dma((groups,))] * 2
        + [dma((2,))] * 2
        + [dma(())],
        compiler_params=pltpu.CompilerParams(
            vmem_limit_bytes=56 * 1024 * 1024, collective_id=0, has_side_effects=True
        ),
        name="belt",
    )(first * PITCH, second * PITCH, rate_coeff, table, wind, natural)
    return (
        out.reshape(count, total * BLOCKS, columns, LANES).transpose(0, 2, 1, 3).reshape(tracers.shape)
    )


def solution(mesh):
    in_specs = (P("tracer", "region", None), P(None, "region", "tracer"), P(), P(), P(), P())
    out_specs = P("tracer", "region", None)
    return jax.shard_map(body, mesh=mesh, in_specs=in_specs, out_specs=out_specs, check_vma=False)
```

profile of v0, /device:TPU:1, one launch (start us, length us, event | category | flops | bytes accessed | tf_op | source)
XLA Modules:
  0.0 219.4 jit_solution(4956676384774783736)
XLA Ops:
  0.0 1.3 broadcast_multiply_fusion.1
  1.3 1.3 broadcast_multiply_fusion
  2.6 1.1 subtract_convert_fusion.table_ref
  3.7 209.8 %belt.1 = f32[128,16,3,2,128]{4,3,2,1,0:T(2,128)} custom-call(s32[1024]{0:T(1024)} %get-tuple-element.7.first_ref, s32[1024]{0:T(1024)} %get-tuple-element.5.second_ref, f32[1024]{0:T(1024)} %rate_ref.1, bf16[256,1024]{1,0:T(8,128)(2,1)} %subtract_convert_fusion.table_ref, f32[2,8,3,2,128]{4,3,2,1,0:T(2,128)} %bitcast.17, f32[128,16,3,2,128]{4,3,2,1,0:T(2,128)} %bitcast.16), custom_call_target="tpu_custom_call" | custom-call | tf_op jit(solution)/shard_map/belt/pallas_call | solution.py:360
  213.5 5.9 %copy.11 = f32[128,2,6144]{2,1,0:T(2,128)} copy(f32[128,2,6144]{2,1,0:T(2,128)} %bitcast.15) | data formatting | bytes 12582912
where the time goes:
time: 220 us; the launch traced here: 219 us
  Pallas kernels  210 us (95%)
  local copies, waits for them, and re-layouts  5.93 us (3%)
  other arithmetic  3.72 us (2%)
    pallas_call x1, Pallas kernels, body(): pl.pallas_call(functools.partial(kernel, parts, count, groups), out_shape...  210 us
    unnamed x1, local copies, waits for them, and re-layouts  5.93 us

commit v1 on v0

v1 whole, which is shorter than its diff:
```python
import functools

import jax
import jax.numpy as jnp
from jax import lax
from jax.experimental import pallas as pl
from jax.experimental.pallas import tpu as pltpu
from jax.sharding import PartitionSpec as P

NY = 48
SUBSTEPS = 4
LANES = 128
BLOCKS = 3
COLUMNS = 2
ROWS = COLUMNS * BLOCKS
GROUP = BLOCKS * LANES
SIDES = 2
STRIP = SIDES * ROWS
PITCH = STRIP + 1
UNROLL = 16
MESH = pl.DeviceIdType.MESH


def south_of(values, lane):
    shifted = []
    for t in range(BLOCKS):
        source = values[t] if t == 0 else jnp.where(lane == LANES - 1, values[t - 1], values[t])
        shifted.append(pltpu.roll(source, 1, 1))
    return shifted


def north_of(values, lane):
    shifted = []
    for t in range(BLOCKS):
        last = t == BLOCKS - 1
        source = values[t] if last else jnp.where(lane == 0, values[t + 1], values[t])
        shifted.append(pltpu.roll(source, LANES - 1, 1))
    return shifted


def up(values):
    return jnp.maximum(values, 0.0)


def down(values):
    return jnp.minimum(values, 0.0)


def write_coefficients(groups, coef_ref, own_ref, west_ref, east_ref):
    lane = lax.broadcasted_iota(jnp.int32, (groups, LANES), 1)

    def read(ref, axis, column):
        rows = ref.reshape(2 * groups * ROWS, LANES)
        return [
            rows[pl.ds(axis * groups * ROWS + t * COLUMNS + column, groups, stride=ROWS), :]
            for t in range(BLOCKS)
        ]

    sources = [(west_ref, COLUMNS - 1)]
    sources += [(own_ref.at[side], column) for side in range(SIDES) for column in range(COLUMNS)]
    sources += [(east_ref, 0), (east_ref, 1)]
    u = [read(ref, 0, column) for ref, column in sources]
    for at in range(len(sources) - 1):
        v = read(sources[at][0], 1, sources[at][1])
        above = north_of(v, lane)
        for t in range(BLOCKS):
            y = (lane + t * LANES) % NY
            bottom, top = y == 0, y == NY - 1
            west_face, east_face = u[at][t], u[at + 1][t]
            center = (
                1.0
                + down(west_face)
                - up(east_face)
                + jnp.where(bottom, 0.0, down(v[t]))
                - jnp.where(top, 0.0, up(above[t]))
            )
            south = jnp.where(bottom, 0.0, up(v[t]))
            north = jnp.where(top, 0.0, -down(above[t]))
            for m, value in enumerate((center, up(west_face), -down(east_face), south, north)):
                coef_ref[(at * BLOCKS + t) * 5 + m, pl.ds(0, groups), :] = value


def kernel(
    parts,
    count,
    groups,
    first_ref,
    second_ref,
    rate_ref,
    first_row,
    second_row,
    product_row,
    flux_ref,
    nat_ref,
    out_ref,
    own_ref,
    stage_ref,
    west_ref,
    east_ref,
    flux_own,
    flux_west,
    flux_east,
    coef_ref,
    now_ref,
    c_ref,
    w_ref,
    k_ref,
    table_ref,
    first_at,
    second_at,
    g_send,
    g_recv,
    r_send,
    r_recv,
    w_send,
    w_recv,
    e_send,
    e_recv,
    f_send,
    f_recv,
    fh_send,
    fh_recv,
):
    region, me = lax.axis_index("region"), lax.axis_index("tracer")
    strips = lax.axis_size("region") // SIDES
    quad, bit, side = region // 4, (region // 2) % 2, region % 2
    strip = quad * 2 + side
    home = side == bit
    reactions = first_ref.shape[0]
    species = parts * count
    rows = count * ROWS

    def seat(at, b):
        return (at // 2) * 4 + b * 2 + at % 2

    west, east = seat((strip + strips - 1) % strips, bit), seat((strip + 1) % strips, bit)
    outer = jnp.where(side == 0, west, east)

    barrier = pltpu.get_barrier_semaphore()
    for shift in range(parts):
        for d in range(2):
            for e in range(2):
                if shift or d or e:
                    pl.semaphore_signal(
                        barrier,
                        1,
                        device_id=(quad * 4 + (bit + d) % 2 * 2 + (side + e) % 2, (me + shift) % parts),
                        device_id_type=MESH,
                    )
    pl.semaphore_signal(barrier, 1, device_id=(outer, me), device_id_type=MESH)
    pl.semaphore_wait(barrier, 4 * parts)

    def remote(source, target, send, recv, device):
        return pltpu.make_async_remote_copy(
            src_ref=source,
            dst_ref=target,
            send_sem=send,
            recv_sem=recv,
            device_id=device,
            device_id_type=MESH,
        )

    def start(copy_here, copy_there, maybe_here):
        if maybe_here:

            @pl.when(home)
            def _():
                copy_here().start()

            @pl.when(jnp.logical_not(home))
            def _():
                copy_there().start()

        else:
            copy_there().start()

    def sent(copy_there, maybe_here):
        if maybe_here:

            @pl.when(jnp.logical_not(home))
            def _():
                copy_there().wait_send()

        else:
            copy_there().wait_send()

    def gather(shift, d, g):
        owner, half = (me + shift) % parts, (bit + d) % 2
        source = nat_ref.at[:, (owner * 2 + half) * groups + g]
        target, arrived = own_ref.at[me, side, g], g_recv.at[me, side, g]
        return (
            lambda: pltpu.make_async_copy(source, target, arrived),
            lambda: remote(source, target, g_send.at[shift, d, g], arrived, (seat(quad * 2 + bit, half), owner)),
            shift == 0 and d == 0,
        )

    def gathered(part, s, g):
        return remote(
            own_ref.at[part, s, g], own_ref.at[part, s, g], g_send.at[0, 0, g], g_recv.at[part, s, g], (east, me)
        )

    def to_west(part, g):
        return remote(
            own_ref.at[part, 0, g], east_ref.at[part, g], e_send.at[part, g], e_recv.at[part, g], (west, me)
        )

    def to_east(part, g):
        return remote(
            own_ref.at[part, 1, g], west_ref.at[part, g], w_send.at[part, g], w_recv.at[part, g], (east, me)
        )

    def give_back(shift, e, g):
        part, s = (me + parts - shift) % parts, (side + e) % 2
        source, target = stage_ref.at[part, s, g], out_ref.at[:, (me * 2 + bit) * groups + g]
        arrived = r_recv.at[shift, (bit + side) % 2, g]
        return (
            lambda: pltpu.make_async_copy(source, target, arrived),
            lambda: remote(source, target, r_send.at[shift, e, g], arrived, (quad * 4 + side * 2 + s, part)),
            shift == 0 and e == 0,
        )

    def returned(shift, d, g):
        target = out_ref.at[:, g]
        return remote(stage_ref.at[0, 0, g], target, r_send.at[0, 0, g], r_recv.at[shift, d, g], (east, me))

    pairs = [(shift, d) for shift in (*range(1, parts), 0) for d in (1, 0)]

    def flux_gather(d):
        half = (bit + d) % 2
        source = flux_ref.at[:, pl.ds(half * groups, groups)]
        target, arrived = flux_own.at[side], f_recv.at[side]
        return (
            lambda: pltpu.make_async_copy(source, target, arrived),
            lambda: remote(source, target, f_send.at[d], arrived, (seat(quad * 2 + bit, half), me)),
            d == 0,
        )

    def flux_gathered(s):
        return remote(flux_own.at[s], flux_own.at[s], f_send.at[0], f_recv.at[s], (east, me))

    def flux_halo():
        return (
            remote(flux_own.at[0], flux_east, fh_send.at[0], fh_recv.at[0], (west, me)),
            remote(flux_own.at[1], flux_west, fh_send.at[1], fh_recv.at[1], (east, me)),
        )

    def pass_on(g):
        for shift in range(parts):
            part = (me + shift) % parts
            for s, onward in ((0, to_west), (1, to_east)):
                gathered(part, s, g).wait_recv()
                onward(part, g).start()

    for d in (1, 0):
        start(*flux_gather(d))
    for g in range(groups):
        for pair in pairs:
            start(*gather(*pair, g))

    def prepare(r, carry):
        first_at[r] = first_ref[r] * PITCH
        second_at[r] = second_ref[r] * PITCH
        k_ref[pl.ds(r, 1), :] = jnp.full((1, LANES), rate_ref[r], jnp.float32)
        return carry

    lax.fori_loop(0, reactions, prepare, 0)

    def build(i, carry):
        at = pl.multiple_of(i * 16, 16)
        order = lax.broadcasted_iota(jnp.int32, (16, reactions), 0) + at
        table_ref[pl.ds(at, 16), :] = (
            (product_row[...] == order).astype(jnp.float32)
            - (first_row[...] == order).astype(jnp.float32)
            - (second_row[...] == order).astype(jnp.float32)
        ).astype(jnp.bfloat16)
        return carry

    lax.fori_loop(0, species // 16, build, 0)

    for s in range(SIDES):
        flux_gathered(s).wait_recv()
    for copy in flux_halo():
        copy.start()
    for copy in flux_halo():
        copy.wait()
    for d in (1, 0):
        _, there, maybe_here = flux_gather(d)
        sent(there, maybe_here)
    write_coefficients(groups, coef_ref, flux_own, flux_west, flux_east)
    pass_on(0)

    lane = lax.broadcasted_iota(jnp.int32, (8, LANES), 1)
    batch = max(b for b in (1, 2, 4) if count % (8 * b) == 0)

    def one_group(g, carry):
        def spread(i, carry):
            now_ref[i, :, :] = coef_ref[i, pl.ds(g, 8, stride=0), :]
            return carry

        lax.fori_loop(0, coef_ref.shape[0], spread, 0)
        for part in range(parts):
            to_west(part, g).wait_recv()
            to_east(part, g).wait_recv()

        def step(cols, at, shifted):
            south, north = shifted
            return [
                now_ref[(at * BLOCKS + t) * 5, :, :] * cols[1][t]
                + now_ref[(at * BLOCKS + t) * 5 + 1, :, :] * cols[0][t]
                + now_ref[(at * BLOCKS + t) * 5 + 2, :, :] * cols[2][t]
                + now_ref[(at * BLOCKS + t) * 5 + 3, :, :] * south[t]
                + now_ref[(at * BLOCKS + t) * 5 + 4, :, :] * north[t]
                for t in range(BLOCKS)
            ]

        width = SIDES * COLUMNS
        for part in range(parts):
            slabs = [west_ref.at[part, g]]
            slabs += [own_ref.at[part, s, g] for s in range(SIDES)]
            slabs += [east_ref.at[part, g]]

            def advect(i, carry, part=part, slabs=slabs):
                def read(slab, column, block):
                    flat = slab.reshape(rows, LANES)
                    return [
                        flat[pl.ds(block * (8 * ROWS) + t * COLUMNS + column, 8, stride=ROWS), :]
                        for t in range(BLOCKS)
                    ]

                def shifts(values):
                    return south_of(values, lane), north_of(values, lane)

                blocks = [i * batch + j for j in range(batch)]
                cols = [
                    [read(slab, column, block) for slab in slabs for column in range(COLUMNS)]
                    for block in blocks
                ]
                moved = [[shifts(c[at + 1]) for at in range(width + 2)] for c in cols]
                mid = [
                    [step(c[at : at + 3], at, m[at]) for at in range(width + 2)]
                    for c, m in zip(cols, moved)
                ]
                moved = [[shifts(c[at + 1]) for at in range(width)] for c in mid]
                for block, c, m in zip(blocks, mid, moved):
                    for at in range(width):
                        new = step(c[at : at + 3], at + 1, m[at])
                        for t in range(BLOCKS):
                            place = at // COLUMNS * ROWS + t * COLUMNS + at % COLUMNS
                            begin = (part * count + block * 8) * PITCH + place
                            c_ref[pl.ds(begin, 8, stride=PITCH), :] = new[t]
                return carry

            lax.fori_loop(0, count // (8 * batch), advect, 0)

        @pl.when(g + 1 < groups)
        def _():
            pass_on(g + 1)

        def react(repeat, carry):
            def velocities(i, carry):
                for j in range(UNROLL):
                    r = i * UNROLL + j
                    one, two = first_at[r], second_at[r]
                    for at in (0, STRIP - 8):
                        w_ref[pl.ds(r * PITCH + at, 8), :] = (
                            c_ref[pl.ds(one + at, 8), :] * c_ref[pl.ds(two + at, 8), :]
                        )
                return carry

            lax.fori_loop(0, reactions // UNROLL, velocities, 0)

            for k in range(STRIP):
                w = w_ref[pl.ds(k, reactions, stride=PITCH), :] * k_ref[...]
                high = w.astype(jnp.bfloat16)
                low = (w - high.astype(jnp.float32)).astype(jnp.bfloat16)
                change = jnp.dot(
                    table_ref[...],
                    jnp.concatenate([high, low], axis=1),
                    preferred_element_type=jnp.float32,
                )
                where = pl.ds(k, species, stride=PITCH)
                c_ref[where, :] = c_ref[where, :] + (change[:, :LANES] + change[:, LANES:])
            return carry

        lax.fori_loop(0, SUBSTEPS, react, 0)

        for part in range(parts):

            def put(i, carry, part=part):
                for s in range(SIDES):
                    flat = stage_ref.at[part, s, g].reshape(rows, LANES)
                    for k in range(ROWS):
                        begin = (part * count + i * 8) * PITCH + s * ROWS + k
                        flat[pl.ds(i * (8 * ROWS) + k, 8, stride=ROWS), :] = c_ref[
                            pl.ds(begin, 8, stride=PITCH), :
                        ]
                return carry

            lax.fori_loop(0, count // 8, put, 0)
        for pair in pairs:
            start(*give_back(*pair, g))
        return carry

    lax.fori_loop(0, groups, one_group, 0)

    def finish(g, carry):
        for pair in pairs:
            for _, there, maybe_here in (gather(*pair, g), give_back(*pair, g)):
                sent(there, maybe_here)
            returned(*pair, g).wait_recv()
        for part in range(parts):
            to_west(part, g).wait_send()
            to_east(part, g).wait_send()
        return carry

    lax.fori_loop(0, groups, finish, 0)


def body(tracers, fluxes, rate_coeff, first_reactant, second_reactant, product_species):
    parts = lax.axis_size("tracer")
    count, columns, length = tracers.shape
    total = length // GROUP
    groups = total // (2 * parts)
    species = parts * count
    reactions = rate_coeff.shape[0]

    def by_block(values):
        lead = values.shape[0]
        blocks = values.shape[2] // LANES
        return (
            values.reshape(lead, columns, blocks, LANES)
            .transpose(0, 2, 1, 3)
            .reshape(lead, blocks // BLOCKS, BLOCKS, columns, LANES)
        )

    natural = by_block(tracers)
    smem = pl.BlockSpec(memory_space=pltpu.SMEM)
    vmem = pl.BlockSpec(memory_space=pltpu.VMEM)
    anywhere = pl.BlockSpec(memory_space=pl.ANY)
    tile = (BLOCKS, columns, LANES)
    f32 = jnp.float32
    dma = pltpu.SemaphoreType.DMA
    coefs = (SIDES * columns + 2) * BLOCKS * 5
    out = pl.pallas_call(
        functools.partial(kernel, parts, count, groups),
        out_shape=jax.ShapeDtypeStruct(natural.shape, f32),
        in_specs=[smem] * 3 + [vmem] * 3 + [anywhere] * 2,
        out_specs=anywhere,
        scratch_shapes=[pltpu.VMEM((parts, SIDES, groups, count, *tile), f32)] * 2
        + [pltpu.VMEM((parts, groups, count, *tile), f32)] * 2
        + [pltpu.VMEM((SIDES, 2, groups, *tile), f32)]
        + [pltpu.VMEM((2, groups, *tile), f32)] * 2
        + [
            pltpu.VMEM((coefs, -(-groups // 8) * 8, LANES), f32),
            pltpu.VMEM((coefs, 8, LANES), f32),
            pltpu.VMEM((species * PITCH + 8, LANES), f32),
            pltpu.VMEM((reactions * PITCH + 8, LANES), f32),
            pltpu.VMEM((reactions, LANES), f32),
            pltpu.VMEM((species, reactions), jnp.bfloat16),
            pltpu.SMEM((reactions,), jnp.int32),
            pltpu.SMEM((reactions,), jnp.int32),
        ]
        + [dma((parts, 2, groups))] * 4
        + [dma((parts, groups))] * 4
        + [dma((2,))] * 4,
        compiler_params=pltpu.CompilerParams(
            vmem_limit_bytes=56 * 1024 * 1024, collective_id=0, has_side_effects=True
        ),
        name="belt",
    )(
        first_reactant,
        second_reactant,
        rate_coeff,
        first_reactant[None, :],
        second_reactant[None, :],
        product_species[None, :],
        by_block(fluxes),
        natural,
    )
    return (
        out.reshape(count, total * BLOCKS, columns, LANES).transpose(0, 2, 1, 3).reshape(tracers.shape)
    )


def solution(mesh):
    in_specs = (P("tracer", "region", None), P(None, "region", "tracer"), P(), P(), P(), P())
    out_specs = P("tracer", "region", None)
    return jax.shard_map(body, mesh=mesh, in_specs=in_specs, out_specs=out_specs, check_vma=False)
```

time: 220 us -> 156 us (0.71)
  the two profiles are of different devices: /device:TPU:1 before, /device:TPU:0 now
where the time goes in v1:
time: 156 us
  Pallas kernels  150 us (96%)
  local copies, waits for them, and re-layouts  5.93 us (4%)
    pallas_call x1, Pallas kernels, body(): pl.pallas_call(functools.partial(kernel, parts, count, groups), out_shape...  150 us
    unnamed x1, local copies, waits for them, and re-layouts  5.93 us

profile of v1, /device:TPU:0, one launch (start us, length us, event | category | flops | bytes accessed | tf_op | source)
XLA Modules:
  0.0 156.1 jit_solution(12330308449603089721)
XLA Ops:
  0.0 150.1 %belt.1 = f32[128,16,3,2,128]{4,3,2,1,0:T(2,128)} custom-call(s32[1024]{0:T(1024)} %first_ref.1, s32[1024]{0:T(1024)} %second_ref.1, f32[1024]{0:T(1024)} %rate_ref.1, s32[1,1024]{1,0:T(1,128)} %bitcast.21, s32[1,1024]{1,0:T(1,128)} %bitcast.22, s32[1,1024]{1,0:T(1,128)} %bitcast.23, f32[2,8,3,2,128]{4,3,2,1,0:T(2,128)} %bitcast.20, ...), custom_call_target="tpu_custom_call" | custom-call | tf_op jit(solution)/shard_map/belt/pallas_call | solution.py:444
  150.1 5.9 %copy.11 = f32[128,2,6144]{2,1,0:T(2,128)} copy(f32[128,2,6144]{2,1,0:T(2,128)} %bitcast.18) | data formatting | bytes 12582912

commit v2 on v1

--- a/solution.py
+++ b/solution.py
@@ -17,7 +17,7 @@
 SIDES = 2
 STRIP = SIDES * ROWS
 PITCH = STRIP + 1
-UNROLL = 16
+UNROLL = 32
 MESH = pl.DeviceIdType.MESH
 
 
@@ -253,9 +253,23 @@
 
     for d in (1, 0):
         start(*flux_gather(d))
+    straight = [pair for pair in pairs if pair[0] and not pair[1]]
+    far = [pair for pair in pairs if pair[0] and pair[1]]
     for g in range(groups):
+
+        @pl.when(side == 0)
+        def _(g=g):
+            for pair in far + straight:
+                start(*gather(*pair, g))
+
+        @pl.when(side != 0)
+        def _(g=g):
+            for pair in straight + far:
+                start(*gather(*pair, g))
+
         for pair in pairs:
-            start(*gather(*pair, g))
+            if pair not in far and pair not in straight:
+                start(*gather(*pair, g))
 
     def prepare(r, carry):
         first_at[r] = first_ref[r] * PITCH

time: 156 us -> 151 us (0.968)
  the two profiles are of different devices: /device:TPU:0 before, /device:TPU:1 now
where the time goes in v2:
time: 151 us; the launch traced here: 150 us
  Pallas kernels  144 us (95%)
  local copies, waits for them, and re-layouts  5.93 us (4%)
    pallas_call x1, Pallas kernels, body(): pl.pallas_call(functools.partial(kernel, parts, count, groups), out_shape...  144 us
    unnamed x1, local copies, waits for them, and re-layouts  5.93 us

profile of v2, /device:TPU:1, one launch (start us, length us, event | category | flops | bytes accessed | tf_op | source)
XLA Modules:
  0.0 149.9 jit_solution(12345327803620474051)
XLA Ops:
  0.0 144.0 %belt.1 = f32[128,16,3,2,128]{4,3,2,1,0:T(2,128)} custom-call(s32[1024]{0:T(1024)} %first_ref.1, s32[1024]{0:T(1024)} %second_ref.1, f32[1024]{0:T(1024)} %rate_ref.1, s32[1,1024]{1,0:T(1,128)} %bitcast.21, s32[1,1024]{1,0:T(1,128)} %bitcast.22, s32[1,1024]{1,0:T(1,128)} %bitcast.23, f32[2,8,3,2,128]{4,3,2,1,0:T(2,128)} %bitcast.20, ...), custom_call_target="tpu_custom_call" | custom-call | tf_op jit(solution)/shard_map/belt/pallas_call | solution.py:458
  144.0 5.9 %copy.11 = f32[128,2,6144]{2,1,0:T(2,128)} copy(f32[128,2,6144]{2,1,0:T(2,128)} %bitcast.18) | data formatting | bytes 12582912

commit v3 on v2

--- a/solution.py
+++ b/solution.py
@@ -459,7 +459,7 @@
         functools.partial(kernel, parts, count, groups),
         out_shape=jax.ShapeDtypeStruct(natural.shape, f32),
         in_specs=[smem] * 3 + [vmem] * 3 + [anywhere] * 2,
-        out_specs=anywhere,
+        out_specs=vmem,
         scratch_shapes=[pltpu.VMEM((parts, SIDES, groups, count, *tile), f32)] * 2
         + [pltpu.VMEM((parts, groups, count, *tile), f32)] * 2
         + [pltpu.VMEM((SIDES, 2, groups, *tile), f32)]
@@ -478,18 +478,23 @@
         + [dma((parts, groups))] * 4
         + [dma((2,))] * 4,
         compiler_params=pltpu.CompilerParams(
-            vmem_limit_bytes=56 * 1024 * 1024, collective_id=0, has_side_effects=True
+            vmem_limit_bytes=45 * 1024 * 1024, collective_id=0, has_side_effects=True
         ),
         name="belt",
     )(
-        first_reactant,
-        second_reactant,
-        rate_coeff,
-        first_reactant[None, :],
-        second_reactant[None, :],
-        product_species[None, :],
-        by_block(fluxes),
-        natural,
+        *[
+            pltpu.with_memory_space_constraint(x, pltpu.HBM)
+            for x in (
+                first_reactant,
+                second_reactant,
+                rate_coeff,
+                first_reactant[None, :],
+                second_reactant[None, :],
+                product_species[None, :],
+                by_block(fluxes),
+                natural,
+            )
+        ]
     )
     return (
         out.reshape(count, total * BLOCKS, columns, LANES).transpose(0, 2, 1, 3).reshape(tracers.shape)

time: 151 us -> 148 us (0.980)
  local copies, waits for them, and re-layouts: 5.93 us -> 2.71 us
    unnamed x1, local copies, waits for them, and re-layouts: 5.93 us -> 2.71 us
where the time goes in v3:
time: 148 us; the launch traced here: 147 us
  Pallas kernels  144 us (97%)
  local copies, waits for them, and re-layouts  2.71 us (2%)
    pallas_call x1, Pallas kernels, body(): pl.pallas_call(functools.partial(kernel, parts, count, groups), out_shape...  144 us

profile of v3, /device:TPU:1, one launch (start us, length us, event | category | flops | bytes accessed | tf_op | source)
XLA Modules:
  0.0 146.6 jit_solution(4880802906802781807)
XLA Ops:
  0.0 143.9 %belt.1 = f32[128,16,3,2,128]{4,3,2,1,0:T(2,128)S(1)} custom-call(s32[1024]{0:T(1024)} %first_ref.1, s32[1024]{0:T(1024)} %second_ref.1, f32[1024]{0:T(1024)} %rate_ref.1, s32[1,1024]{1,0:T(1,128)} %bitcast.21, s32[1,1024]{1,0:T(1,128)} %bitcast.22, s32[1,1024]{1,0:T(1,128)} %bitcast.23, f32[2,8,3,2,128]{4,3,2,1,0:T(2,128)} %bitcast.20, ...), custom_call_target="tpu_custom_call" | custom-call | tf_op jit(solution)/shard_map/belt/pallas_call | solution.py:458
  143.9 2.7 %copy.11 = f32[128,2,6144]{2,1,0:T(2,128)} copy(f32[128,2,6144]{2,1,0:T(2,128)S(1)} %bitcast.18) | data formatting | bytes 12582912

commit v4 on v3

--- a/solution.py
+++ b/solution.py
@@ -244,9 +244,9 @@
             remote(flux_own.at[1], flux_west, fh_send.at[1], fh_recv.at[1], (east, me)),
         )
 
-    def pass_on(g):
-        for shift in range(parts):
-            part = (me + shift) % parts
+    def pass_on(g, shifts):
+        for shift in shifts:
+            part = (me + shift + jnp.where(home, 0, 1)) % parts
             for s, onward in ((0, to_west), (1, to_east)):
                 gathered(part, s, g).wait_recv()
                 onward(part, g).start()
@@ -301,7 +301,7 @@
         _, there, maybe_here = flux_gather(d)
         sent(there, maybe_here)
     write_coefficients(groups, coef_ref, flux_own, flux_west, flux_east)
-    pass_on(0)
+    pass_on(0, range(parts))
 
     lane = lax.broadcasted_iota(jnp.int32, (8, LANES), 1)
     batch = max(b for b in (1, 2, 4) if count % (8 * b) == 0)
@@ -312,10 +312,6 @@
             return carry
 
         lax.fori_loop(0, coef_ref.shape[0], spread, 0)
-        for part in range(parts):
-            to_west(part, g).wait_recv()
-            to_east(part, g).wait_recv()
-
         def step(cols, at, shifted):
             south, north = shifted
             return [
@@ -328,7 +324,10 @@
             ]
 
         width = SIDES * COLUMNS
-        for part in range(parts):
+        for shift in range(parts):
+            part = (me + shift + jnp.where(home, 0, 1)) % parts
+            to_west(part, g).wait_recv()
+            to_east(part, g).wait_recv()
             slabs = [west_ref.at[part, g]]
             slabs += [own_ref.at[part, s, g] for s in range(SIDES)]
             slabs += [east_ref.at[part, g]]
@@ -368,7 +367,7 @@
 
         @pl.when(g + 1 < groups)
         def _():
-            pass_on(g + 1)
+            pass_on(g + 1, range(parts - 1))
 
         def react(repeat, carry):
             def velocities(i, carry):
@@ -394,6 +393,11 @@
                 )
                 where = pl.ds(k, species, stride=PITCH)
                 c_ref[where, :] = c_ref[where, :] + (change[:, :LANES] + change[:, LANES:])
+
+            @pl.when(jnp.logical_and(repeat == 0, g + 1 < groups))
+            def _():
+                pass_on(g + 1, range(parts - 1, parts))
+
             return carry
 
         lax.fori_loop(0, SUBSTEPS, react, 0)

time: 148 us -> 147 us (level)
  Pallas kernels: 144 us -> 142 us
    pallas_call x1, Pallas kernels: 144 us -> 142 us  [body(): pl.pallas_call(functools.partial(kernel, parts, count, groups), out_shape...]
where the time goes in v4:
time: 147 us; the launch traced here: 144 us
  Pallas kernels  142 us (97%)
  local copies, waits for them, and re-layouts  2.71 us (2%)
    pallas_call x1, Pallas kernels, body(): pl.pallas_call(functools.partial(kernel, parts, count, groups), out_shape...  142 us

profile of v4, /device:TPU:1, one launch (start us, length us, event | category | flops | bytes accessed | tf_op | source)
XLA Modules:
  0.0 144.4 jit_solution(14760205595535798648)
XLA Ops:
  0.0 141.7 %belt.1 = f32[128,16,3,2,128]{4,3,2,1,0:T(2,128)S(1)} custom-call(s32[1024]{0:T(1024)} %first_ref.1, s32[1024]{0:T(1024)} %second_ref.1, f32[1024]{0:T(1024)} %rate_ref.1, s32[1,1024]{1,0:T(1,128)} %bitcast.21, s32[1,1024]{1,0:T(1,128)} %bitcast.22, s32[1,1024]{1,0:T(1,128)} %bitcast.23, f32[2,8,3,2,128]{4,3,2,1,0:T(2,128)} %bitcast.20, ...), custom_call_target="tpu_custom_call" | custom-call | tf_op jit(solution)/shard_map/belt/pallas_call | solution.py:462
  141.7 2.7 %copy.11 = f32[128,2,6144]{2,1,0:T(2,128)} copy(f32[128,2,6144]{2,1,0:T(2,128)S(1)} %bitcast.18) | data formatting | bytes 12582912

commit v5 on v4

--- a/solution.py
+++ b/solution.py
@@ -415,7 +415,7 @@
                 return carry
 
             lax.fori_loop(0, count // 8, put, 0)
-        for pair in pairs:
+        for pair in reversed(pairs):
             start(*give_back(*pair, g))
         return carry
 

time: 147 us -> 146 us (level); the launches traced: 144 us -> 146 us
    pallas_call x1, Pallas kernels: 142 us -> 143 us  [body(): pl.pallas_call(functools.partial(kernel, parts, count, groups), out_shape...]
where the time goes in v5:
time: 146 us
  Pallas kernels  143 us (98%)
  local copies, waits for them, and re-layouts  2.71 us (2%)
    pallas_call x1, Pallas kernels, body(): pl.pallas_call(functools.partial(kernel, parts, count, groups), out_shape...  143 us

profile of v5, /device:TPU:1, one launch (start us, length us, event | category | flops | bytes accessed | tf_op | source)
XLA Modules:
  0.0 146.0 jit_solution(12562053113810284659)
XLA Ops:
  0.0 143.3 %belt.1 = f32[128,16,3,2,128]{4,3,2,1,0:T(2,128)S(1)} custom-call(s32[1024]{0:T(1024)} %first_ref.1, s32[1024]{0:T(1024)} %second_ref.1, f32[1024]{0:T(1024)} %rate_ref.1, s32[1,1024]{1,0:T(1,128)} %bitcast.21, s32[1,1024]{1,0:T(1,128)} %bitcast.22, s32[1,1024]{1,0:T(1,128)} %bitcast.23, f32[2,8,3,2,128]{4,3,2,1,0:T(2,128)} %bitcast.20, ...), custom_call_target="tpu_custom_call" | custom-call | tf_op jit(solution)/shard_map/belt/pallas_call | solution.py:462
  143.3 2.7 %copy.11 = f32[128,2,6144]{2,1,0:T(2,128)} copy(f32[128,2,6144]{2,1,0:T(2,128)S(1)} %bitcast.18) | data formatting | bytes 12582912

commit v6 on v5

--- a/solution.py
+++ b/solution.py
@@ -247,7 +247,7 @@
     def pass_on(g, shifts):
         for shift in shifts:
             part = (me + shift + jnp.where(home, 0, 1)) % parts
-            for s, onward in ((0, to_west), (1, to_east)):
+            for s, onward in ((1, to_east), (0, to_west)):
                 gathered(part, s, g).wait_recv()
                 onward(part, g).start()
 

time: 146 us -> 146 us (level)
  no operation moved by 1% of the time
where the time goes in v6:
time: 146 us
  Pallas kernels  143 us (98%)
  local copies, waits for them, and re-layouts  2.71 us (2%)
    pallas_call x1, Pallas kernels, body(): pl.pallas_call(functools.partial(kernel, parts, count, groups), out_shape...  143 us

profile of v6, /device:TPU:1, one launch (start us, length us, event | category | flops | bytes accessed | tf_op | source)
XLA Modules:
  0.0 145.8 jit_solution(7379752050840905105)
XLA Ops:
  0.0 143.1 %belt.1 = f32[128,16,3,2,128]{4,3,2,1,0:T(2,128)S(1)} custom-call(s32[1024]{0:T(1024)} %first_ref.1, s32[1024]{0:T(1024)} %second_ref.1, f32[1024]{0:T(1024)} %rate_ref.1, s32[1,1024]{1,0:T(1,128)} %bitcast.21, s32[1,1024]{1,0:T(1,128)} %bitcast.22, s32[1,1024]{1,0:T(1,128)} %bitcast.23, f32[2,8,3,2,128]{4,3,2,1,0:T(2,128)} %bitcast.20, ...), custom_call_target="tpu_custom_call" | custom-call | tf_op jit(solution)/shard_map/belt/pallas_call | solution.py:462
  143.1 2.7 %copy.11 = f32[128,2,6144]{2,1,0:T(2,128)} copy(f32[128,2,6144]{2,1,0:T(2,128)S(1)} %bitcast.18) | data formatting | bytes 12582912

commit v7 on v5

--- a/solution.py
+++ b/solution.py
@@ -17,7 +17,7 @@
 SIDES = 2
 STRIP = SIDES * ROWS
 PITCH = STRIP + 1
-UNROLL = 32
+UNROLL = 64
 MESH = pl.DeviceIdType.MESH
 
 

time: 146 us -> 146 us (level)
  no operation moved by 1% of the time
where the time goes in v7:
time: 146 us
  Pallas kernels  143 us (98%)
  local copies, waits for them, and re-layouts  2.71 us (2%)
    pallas_call x1, Pallas kernels, body(): pl.pallas_call(functools.partial(kernel, parts, count, groups), out_shape...  143 us

profile of v7, /device:TPU:1, one launch (start us, length us, event | category | flops | bytes accessed | tf_op | source)
XLA Modules:
  0.0 145.9 jit_solution(1593338818476095278)
XLA Ops:
  0.0 143.2 %belt.1 = f32[128,16,3,2,128]{4,3,2,1,0:T(2,128)S(1)} custom-call(s32[1024]{0:T(1024)} %first_ref.1, s32[1024]{0:T(1024)} %second_ref.1, f32[1024]{0:T(1024)} %rate_ref.1, s32[1,1024]{1,0:T(1,128)} %bitcast.21, s32[1,1024]{1,0:T(1,128)} %bitcast.22, s32[1,1024]{1,0:T(1,128)} %bitcast.23, f32[2,8,3,2,128]{4,3,2,1,0:T(2,128)} %bitcast.20, ...), custom_call_target="tpu_custom_call" | custom-call | tf_op jit(solution)/shard_map/belt/pallas_call | solution.py:462
  143.2 2.7 %copy.11 = f32[128,2,6144]{2,1,0:T(2,128)} copy(f32[128,2,6144]{2,1,0:T(2,128)S(1)} %bitcast.18) | data formatting | bytes 12582912
